TPU v7x, 32 devices: a whole 2x2x4 slice. The times are simulated.
32 devices in a mesh: view: 8 (over z, core), span: 4 (over y, x).
Axes of the slice: x: 2, y: 2, z: 4, core: 2. Of those that a mesh axis runs over, the one named last changes fastest.
Arguments:
- tokens: bfloat16 [8, 1024, 1024], P('view', 'span'), may hold values from -6 to 6
- scan_order: int32 [8, 1024], P('view'), may hold values from 0 to 1023, as said below
- w_merge: bfloat16 [4096, 1024], replicated, may hold values from -0.09375 to 0.09375
- bias: bfloat16 [1024], replicated, may hold values from -4 to 4
- cotangent: bfloat16 [8, 256, 1024], P('view', 'span'), may hold values from -6 to 6
Outputs:
- merged_out: bfloat16 [8, 256, 1024], P('view', 'span')
- token_grad: bfloat16 [8, 1024, 1024], P('view', 'span')
- weight_grad: float32 [4096, 1024], P(('view', 'span'))
- bias_grad: float32 [1024], replicated
Inputs may be any that keep to these rules, and one draw needn't show every extreme that they name: `scan_order`: each row is a permutation of the raster indices of one view. Call tokens 256 * b to 256 * (b + 1) - 1 band b, and scan positions 256 * c to 256 * (c + 1) - 1 block c: every block holds at most 96 tokens of any band, and in every row each block holds exactly 96 tokens of some band.
All inputs are finite; a program needn't handle non-finite values.
Results may differ from a plain program's by a relative error of at most 0.001.
Values may be sent and summed in bfloat16 or wider, within the bound.
No kernel may reach another device: no remote copies, remote signals or barrier semaphores. Data moves between devices by JAX's collectives and lax.ppermute only.
A program may use at most 128 MiB of HBM per device.

v0:
```python
import math
import jax
import jax.numpy as jnp
from jax import lax
from jax.sharding import PartitionSpec as P

COLS = 128


def body(tokens, scan_order, w_merge, bias, cotangent):
    spans = lax.axis_size("span")
    views = lax.axis_size("view")
    span_index = lax.axis_index("span")
    tok_dev = tokens.shape[1]
    width = tokens.shape[2]
    capacity = 3 * (tok_dev // spans) // 2
    rows_dev = tok_dev // COLS
    order_all = scan_order[0].reshape(spans, tok_dev)
    owners = order_all // tok_dev
    owner_hot = (owners[:, :, None] == jnp.arange(spans, dtype=jnp.int32)[None, None, :]).astype(
        jnp.int32
    )
    slot_rank = jnp.sum((jnp.cumsum(owner_hot, axis=1) - 1) * owner_hot, axis=2)
    dest_slots = owners * capacity + slot_rank
    my_slots = lax.dynamic_index_in_dim(dest_slots, span_index, 0, keepdims=False)
    outgoing = jnp.zeros((spans * capacity, width), jnp.bfloat16).at[my_slots].set(tokens[0])
    received = lax.all_to_all(
        outgoing.reshape(spans, capacity, width), "span", split_axis=0, concat_axis=0, tiled=True
    )
    arriving = owners == span_index
    source_slot = jnp.arange(spans, dtype=jnp.int32)[:, None] * capacity + slot_rank
    local_index = jnp.where(arriving, order_all - span_index * tok_dev, tok_dev)
    source_of = (
        jnp.zeros((tok_dev,), jnp.int32)
        .at[local_index.reshape(-1)]
        .set(source_slot.reshape(-1), mode="drop")
    )
    raster = received.reshape(spans * capacity, width)[source_of]
    merged = (
        raster.reshape(rows_dev // 2, 2, COLS // 2, 2, width)
        .transpose(0, 2, 1, 3, 4)
        .reshape(tok_dev // 4, 4 * width)
    )
    merged_out = (
        jnp.dot(merged, w_merge, preferred_element_type=jnp.float32) + bias.astype(jnp.float32)
    ).astype(jnp.bfloat16)
    grads = cotangent[0]
    grad_merged = lax.dot_general(
        grads, w_merge, (((1,), (1,)), ((), ())), preferred_element_type=jnp.float32
    ).astype(jnp.bfloat16)
    grad_raster = (
        grad_merged.reshape(rows_dev // 2, COLS // 2, 2, 2, width)
        .transpose(0, 2, 1, 3, 4)
        .reshape(tok_dev, width)
    )
    going_back = jnp.zeros((spans * capacity, width), jnp.bfloat16).at[source_of].set(grad_raster)
    returned = lax.all_to_all(
        going_back.reshape(spans, capacity, width), "span", split_axis=0, concat_axis=0, tiled=True
    )
    token_grad = returned.reshape(spans * capacity, width)[my_slots]
    kernel_rows = 4 * width
    merged_rows = merged.shape[0]
    group_rows = kernel_rows // (views * spans)
    regrouped = merged.reshape(merged_rows, views, spans, group_rows).transpose(0, 2, 1, 3)
    view_tokens = lax.all_to_all(regrouped, "span", split_axis=1, concat_axis=0, tiled=True)
    view_tokens = view_tokens.reshape(spans * merged_rows, views * group_rows)
    all_grads = lax.all_gather(grads, "span", axis=0, tiled=True)
    partial_sum = lax.dot_general(
        view_tokens, all_grads, (((0,), (0,)), ((), ())), preferred_element_type=jnp.float32
    )
    weight_sum = lax.psum_scatter(partial_sum, "view", scatter_dimension=0, tiled=True)
    bias_total = lax.psum(jnp.sum(grads.astype(jnp.float32), axis=0), ("view", "span"))
    grad_scale = 1.0 / math.sqrt(views * spans * (tok_dev // 4))
    return (merged_out[None], token_grad[None], weight_sum * grad_scale, bias_total * grad_scale)


def solution(mesh):
    in_specs = (P("view", "span", None), P("view", None), P(), P(), P("view", "span", None))
    out_specs = (P("view", "span", None), P("view", "span", None), P(("view", "span"), None), P())
    return jax.shard_map(body, mesh=mesh, in_specs=in_specs, out_specs=out_specs, check_vma=False)
```

profile of v0, /device:TPU:0, one launch (start us, length us, event | category | flops | bytes accessed | tf_op | source)
XLA Modules:
  0.0 131.2 jit_solution(6496516762859729099)
XLA Ops:
  7.2 0.8 and_select_fusion.1
  8.0 4.8 %reduce-window.6 = s32[4,4,2,128]{3,2,1,0:T(2,128)S(1)} reduce-window(s32[4,4,2,128]{3,2,1,0:T(2,128)S(1)} %compare_convert_fusion, s32[]{:T(128)} %constant.19.clone.1), window={size=1x1x1x128 pad=0_0x0_0x0_0x127_0}, to_apply=%region_0.1 | reduce-window | flops 520192 | bytes 32772 | tf_op jit(solution)/shard_map/reduce-window
  12.9 0.1 copy.16
  13.0 0.1 copy.17
  13.2 0.1 add_add_fusion
  13.3 0.5 broadcast.237
  13.8 1.3 %reduce.3 = s32[1024]{0:T(1024)S(1)} reduce(s32[1,1024]{1,0:T(1,128)} %param.6, s32[]{:T(128)} %broadcast.237), dimensions={0}, to_apply=%param.6.reduce_sub_computation.3 | reduce | bytes 8196 | tf_op args[1]
  15.2 2.6 %scatter_custom_fusion = bf16[384,1024]{1,0:T(8,128)(2,1)} fusion(s32[256]{0:T(256)S(1)} %bitcast.75, bf16[1,256,1024]{2,1,0:T(8,128)(2,1)S(1)} %copy-done, bf16[]{:T(256)} %constant.15.clone.1), kind=kCustom, calls=%fused_computation.13 | custom fusion | bytes 1310722 | tf_op jit(solution)/shard_map/scatter | solution.py:26
  17.8 5.2 %all-to-all-start = ((bf16[4,96,1024]{2,1,0:T(8,128)(2,1)}), bf16[4,96,1024]{2,1,0:T(8,128)(2,1)S(1)}, u32[]{:S(2)}, u32[]{:S(2)}) async-start(bf16[4,96,1024]{2,1,0:T(8,128)(2,1)} %bitcast.6), calls=%async_computation | async-start | bytes 1572864 | tf_op jit(solution)/shard_map/all_to_all | solution.py:27
  23.1 0.7 compare_select_fusion
  23.8 4.3 %scatter_custom_fusion.1 = s32[256]{0:T(256)S(1)} fusion(s32[1024]{0:T(1024)S(1)} %bitcast.78, s32[1024]{0:T(1024)S(1)} %bitcast.77, s32[]{:T(128)} %constant.19.clone.1), kind=kCustom, calls=%fused_computation.59 | custom fusion | bytes 1028 | tf_op jit(solution)/shard_map/scatter | solution.py:36
  28.2 5.7 %all-to-all-done = bf16[4,96,1024]{2,1,0:T(8,128)(2,1)S(1)} async-done(((bf16[4,96,1024]{2,1,0:T(8,128)(2,1)}), bf16[4,96,1024]{2,1,0:T(8,128)(2,1)S(1)}, u32[]{:S(2)}, u32[]{:S(2)}) %all-to-all-start) | async-done | bytes 786464 | tf_op jit(solution)/shard_map/all_to_all | solution.py:27
  33.8 1.2 gather_fusion
  35.0 0.2 reshape.224
  35.2 0.4 copy.30
  35.6 0.3 reshape_reshape.3
  35.9 0.9 copy.20
  36.8 3.5 %all-to-all-start.2 = ((bf16[64,4,8,128]{3,2,0,1:T(8,128)(2,1)}), bf16[64,4,8,128]{3,2,0,1:T(8,128)(2,1)S(1)}, u32[]{:S(2)}, u32[]{:S(2)}) async-start(bf16[64,4,8,128]{3,2,0,1:T(8,128)(2,1)} %copy.20), calls=%async_computation.2 | async-start | bytes 1048576 | tf_op jit(solution)/shard_map/all_to_all | solution.py:65
  40.3 13.7 %all-gather = bf16[1,256,1024]{2,1,0:T(8,128)(2,1)S(1)} all-gather(bf16[1,64,1024]{2,1,0:T(8,128)(2,1)S(1)} %copy-done.1), channel_id=2, replica_groups=mesh['view'=8,'span'=4] {'span'}, dimensions={1}, use_global_device_ids=true | all-gather | bytes 655360 | tf_op jit(solution)/shard_map/all_gather | solution.py:67
  54.0 2.7 %fusion.2 = f32[1024,1024]{1,0:T(8,128)} fusion(bf16[32,8,8,128]{3,2,1,0:T(8,128)(2,1)S(1)} %bitcast.70, bf16[1,256,1024]{2,1,0:T(8,128)(2,1)S(1)} %all-gather), kind=kOutput, calls=%fused_computation.9 | convolution fusion | flops 536870912 | bytes 5242880 | tf_op jit(solution)/shard_map/dot_general | solution.py:68
  56.7 6.0 %convolution_convert_fusion = bf16[64,4096]{1,0:T(8,128)(2,1)S(1)} fusion(bf16[4096,1024]{1,0:T(8,128)(2,1)} %param.7, bf16[1,64,1024]{2,1,0:T(8,128)(2,1)S(1)} %copy-done.1), kind=kOutput, calls=%fused_computation.5 | convolution fusion | flops 537133056 | bytes 9043968 | tf_op jit(solution)/shard_map/dot_general | solution.py:48
  62.8 0.4 reshape.226
  63.1 0.4 copy.29
  63.5 0.2 reshape.267
  63.7 2.6 %scatter_custom_fusion.2 = bf16[384,1024]{1,0:T(8,128)(2,1)} fusion(s32[256]{0:T(256)S(1)} %compare_select_fusion.6, bf16[256,1024]{1,0:T(8,128)(2,1)S(1)} %reshape.267, bf16[]{:T(256)} %constant.15.clone.1), kind=kCustom, calls=%fused_computation.17 | custom fusion | bytes 786434 | tf_op jit(solution)/shard_map/scatter | solution.py:56
  66.3 3.5 %all-to-all-start.1 = ((bf16[4,96,1024]{2,1,0:T(8,128)(2,1)}), bf16[4,96,1024]{2,1,0:T(8,128)(2,1)S(1)}, u32[]{:S(2)}, u32[]{:S(2)}) async-start(bf16[4,96,1024]{2,1,0:T(8,128)(2,1)} %bitcast.14), calls=%async_computation.1 | async-start | bytes 1572864 | tf_op jit(solution)/shard_map/all_to_all | solution.py:57
  69.9 44.0 %psum.7 = f32[1024]{0:T(1024)S(1)} all-reduce(f32[1024]{0:T(1024)S(1)} %convert_reduce_fusion), channel_id=1, replica_groups=mesh['view'=8,'span'=4] {'view','span'}, use_global_device_ids=true, to_apply=%region_8.9 | all-reduce | flops 1024 | bytes 8192 | tf_op jit(solution)/shard_map/psum | solution.py:72
  113.8 0.6 broadcast_multiply_fusion.1
  114.4 0.4 reshape.225
  114.8 2.0 %gather_fusion.1 = bf16[256,1024]{1,0:T(8,128)(2,1)} fusion(bf16[384,1024]{1,0:T(8,128)(2,1)S(1)} %bitcast.67, s32[1024]{0:T(1024)S(1)} %pad_clamp_fusion), kind=kCustom, calls=%fused_computation.1 | custom fusion | bytes 1049600 | tf_op jit(solution)/shard_map/gather | solution.py:60
  116.8 5.6 %fusion.1 = bf16[1,64,1024]{2,1,0:T(8,128)(2,1)} fusion(bf16[64,4096]{1,0:T(8,128)(2,1)S(1)} %reshape.225, bf16[4096,1024]{1,0:T(8,128)(2,1)} %param.7, f32[1024]{0:T(1024)S(1)} %convert_element_type.18), kind=kOutput, calls=%fused_computation.8 | convolution fusion | flops 537001984 | bytes 9048064 | tf_op jit(solution)/shard_map/dot_general | solution.py:45
  122.4 1.9 %broadcast_multiply_fusion = f32[128,1024]{1,0:T(8,128)} fusion(f32[128,1024]{1,0:T(8,128)} %reduce-scatter.2.cloned.1.call-done), kind=kLoop, calls=%fused_computation.21 | loop fusion | flops 131072 | bytes 1048576 | tf_op jit(solution)/shard_map/mul | solution.py:74
  (28 shorter events, 0.4 us)
Async XLA Ops:
  7.2 8.1 %copy-start = (bf16[1,256,1024]{2,1,0:T(8,128)(2,1)S(1)}, bf16[1,256,1024]{2,1,0:T(8,128)(2,1)}, u32[]{:S(2)}) copy-start(bf16[1,256,1024]{2,1,0:T(8,128)(2,1)} %param.5) | copy-start | bytes 1572868
  7.2 33.1 %copy-start.1 = (bf16[1,64,1024]{2,1,0:T(8,128)(2,1)S(1)}, bf16[1,64,1024]{2,1,0:T(8,128)(2,1)}, u32[]{:S(2)}) copy-start(bf16[1,64,1024]{2,1,0:T(8,128)(2,1)} %param.9) | copy-start | bytes 393220
  17.8 16.0 %all-to-all-start = ((bf16[4,96,1024]{2,1,0:T(8,128)(2,1)}), bf16[4,96,1024]{2,1,0:T(8,128)(2,1)S(1)}, u32[]{:S(2)}, u32[]{:S(2)}) async-start(bf16[4,96,1024]{2,1,0:T(8,128)(2,1)} %bitcast.6), calls=%async_computation | async-start | bytes 1572864 | tf_op jit(solution)/shard_map/all_to_all | solution.py:27
  36.8 17.2 %all-to-all-start.2 = ((bf16[64,4,8,128]{3,2,0,1:T(8,128)(2,1)}), bf16[64,4,8,128]{3,2,0,1:T(8,128)(2,1)S(1)}, u32[]{:S(2)}, u32[]{:S(2)}) async-start(bf16[64,4,8,128]{3,2,0,1:T(8,128)(2,1)} %copy.20), calls=%async_computation.2 | async-start | bytes 1048576 | tf_op jit(solution)/shard_map/all_to_all | solution.py:65
  40.3 82.2 %reduce-scatter.2.cloned.1.call-start = ((), (), s32[]{:S(2)}) async-start(), calls=%async_computation.4 | async-start | bytes 4718592 | tf_op jit(solution)/shard_map/reduce_scatter | solution.py:71
  56.7 13.1 %copy-start.2 = (bf16[1024]{0:T(1024)(128)(2,1)S(1)}, bf16[1024]{0:T(1024)(128)(2,1)}, u32[]{:S(2)}) copy-start(bf16[1024]{0:T(1024)(128)(2,1)} %param.8) | copy-start | bytes 6148
  66.3 48.5 %all-to-all-start.1 = ((bf16[4,96,1024]{2,1,0:T(8,128)(2,1)}), bf16[4,96,1024]{2,1,0:T(8,128)(2,1)S(1)}, u32[]{:S(2)}, u32[]{:S(2)}) async-start(bf16[4,96,1024]{2,1,0:T(8,128)(2,1)} %bitcast.14), calls=%async_computation.1 | async-start | bytes 1572864 | tf_op jit(solution)/shard_map/all_to_all | solution.py:57
Sparse Core Ops, SparseCore 0:
  56.8 51.2 reduce-scatter.1
where the time goes:
time: 132 us; the launch traced here: 131 us
  blocking collectives  57.6 us (44%)
  local copies, waits for them, and re-layouts  16.6 us (13%)
  matrix products  14.3 us (11%)
  between operations  14.2 us (11%)
  starting transfers between devices  12.2 us (9%)
  other arithmetic  10.4 us (8%)
  waiting for transfers between devices  5.71 us (4%)
    psum x1, blocking collectives, body(): lax.psum(jnp.sum(grads.astype(jnp.float32), axis=0), ('view', 'span'))  44 us
    all_gather x1, blocking collectives, body(): all_grads = lax.all_gather(grads, 'span', axis=0, tiled=True)  13.7 us
    dot_general x1, matrix products, body(): lax.dot_general(grads, w_merge, (((1,), (1,)), ((), ())), preferred_eleme...  6.04 us
    all_to_all x1, waiting for transfers between devices, body(): lax.all_to_all(outgoing.reshape(spans, capacity, width), 'span', split_ax...  5.69 us
    dot_general x1, matrix products, body(): jnp.dot(merged, w_merge, preferred_element_type=jnp.float32)  5.61 us
    all_to_all x1, starting transfers between devices, body(): lax.all_to_all(outgoing.reshape(spans, capacity, width), 'span', split_ax...  5.19 us
    another operation x2, other arithmetic  4.84 us
    scatter x1, local copies, waits for them, and re-layouts, body(): source_of = jnp.zeros((tok_dev,), jnp.int32).at[local_index.reshape(-1)]....  4.3 us
  transfers between devices with their start and end apart: 4, of which 1 were waited for; matrix products, arithmetic and copies ran while one was open for 18% of the time, Pallas kernels for 0%

commit v1 on v0

--- a/solution.py
+++ b/solution.py
@@ -69,7 +69,7 @@
         view_tokens, all_grads, (((0,), (0,)), ((), ())), preferred_element_type=jnp.float32
     )
     weight_sum = lax.psum_scatter(partial_sum, "view", scatter_dimension=0, tiled=True)
-    bias_total = lax.psum(jnp.sum(grads.astype(jnp.float32), axis=0), ("view", "span"))
+    bias_total = lax.psum(lax.psum(jnp.sum(grads.astype(jnp.float32), axis=0), "span"), "view")
     grad_scale = 1.0 / math.sqrt(views * spans * (tok_dev // 4))
     return (merged_out[None], token_grad[None], weight_sum * grad_scale, bias_total * grad_scale)
 

time: 132 us -> 117 us (0.89)
  blocking collectives: 57.6 us -> 39.5 us
  waiting for transfers between devices: 5.71 us -> 8.72 us
    psum x1 -> x2, blocking collectives: 44 us -> 25.8 us  [the longest x1 14.5 us: body(): lax.psum(lax.psum(jnp.sum(grads.astype(jnp.float32), axis=0), 'span'), 'v...]
    reduce_scatter x1, waiting for transfers between devices: 0.01 us -> 3.01 us  [body(): lax.psum_scatter(partial_sum, 'view', scatter_dimension=0, tiled=True)]
  transfers between devices with their start and end apart: 4 -> 4, of which waited for: 1 -> 2; matrix products, arithmetic and copies ran while one was open for 18% -> 20% of each run, Pallas kernels for 0% -> 0%
where the time goes in v1:
time: 117 us; the launch traced here: 116 us
  blocking collectives  39.5 us (34%)
  local copies, waits for them, and re-layouts  16.6 us (14%)
  matrix products  14.4 us (12%)
  between operations  14.2 us (12%)
  starting transfers between devices  12.2 us (10%)
  other arithmetic  10.4 us (9%)
  waiting for transfers between devices  8.72 us (7%)
    psum x1, blocking collectives, body(): lax.psum(lax.psum(jnp.sum(grads.astype(jnp.float32), axis=0), 'span'), 'v...  14.5 us
    all_gather x1, blocking collectives, body(): all_grads = lax.all_gather(grads, 'span', axis=0, tiled=True)  13.7 us
    psum x1, blocking collectives, body(): lax.psum(jnp.sum(grads.astype(jnp.float32), axis=0), 'span')  11.4 us
    dot_general x1, matrix products, body(): lax.dot_general(grads, w_merge, (((1,), (1,)), ((), ())), preferred_eleme...  6.04 us
    dot_general x1, matrix products, body(): jnp.dot(merged, w_merge, preferred_element_type=jnp.float32)  5.69 us
    all_to_all x1, waiting for transfers between devices, body(): lax.all_to_all(outgoing.reshape(spans, capacity, width), 'span', split_ax...  5.69 us
    all_to_all x1, starting transfers between devices, body(): lax.all_to_all(outgoing.reshape(spans, capacity, width), 'span', split_ax...  5.19 us
    another operation x2, other arithmetic  4.84 us
  transfers between devices with their start and end apart: 4, of which 2 were waited for; matrix products, arithmetic and copies ran while one was open for 20% of the time, Pallas kernels for 0%

profile of v1, /device:TPU:0, one launch (start us, length us, event | category | flops | bytes accessed | tf_op | source)
XLA Modules:
  0.0 116.1 jit_solution(15012522365525005192)
XLA Ops:
  7.2 0.8 and_select_fusion.1
  8.0 4.8 %reduce-window.6 = s32[4,4,2,128]{3,2,1,0:T(2,128)S(1)} reduce-window(s32[4,4,2,128]{3,2,1,0:T(2,128)S(1)} %compare_convert_fusion, s32[]{:T(128)} %constant.19.clone.1), window={size=1x1x1x128 pad=0_0x0_0x0_0x127_0}, to_apply=%region_0.1 | reduce-window | flops 520192 | bytes 32772 | tf_op jit(solution)/shard_map/reduce-window
  12.9 0.1 copy.16
  13.3 0.5 broadcast.237
  13.8 1.3 %reduce.3 = s32[1024]{0:T(1024)S(1)} reduce(s32[1,1024]{1,0:T(1,128)} %param.6, s32[]{:T(128)} %broadcast.237), dimensions={0}, to_apply=%param.6.reduce_sub_computation.3 | reduce | bytes 8196 | tf_op args[1]
  15.2 2.6 %scatter_custom_fusion = bf16[384,1024]{1,0:T(8,128)(2,1)} fusion(s32[256]{0:T(256)S(1)} %bitcast.75, bf16[1,256,1024]{2,1,0:T(8,128)(2,1)S(1)} %copy-done, bf16[]{:T(256)} %constant.15.clone.1), kind=kCustom, calls=%fused_computation.13 | custom fusion | bytes 1310722 | tf_op jit(solution)/shard_map/scatter | solution.py:26
  17.8 5.2 %all-to-all-start = ((bf16[4,96,1024]{2,1,0:T(8,128)(2,1)}), bf16[4,96,1024]{2,1,0:T(8,128)(2,1)S(1)}, u32[]{:S(2)}, u32[]{:S(2)}) async-start(bf16[4,96,1024]{2,1,0:T(8,128)(2,1)} %bitcast.6), calls=%async_computation | async-start | bytes 1572864 | tf_op jit(solution)/shard_map/all_to_all | solution.py:27
  23.1 0.7 compare_select_fusion
  23.8 4.3 %scatter_custom_fusion.1 = s32[256]{0:T(256)S(1)} fusion(s32[1024]{0:T(1024)S(1)} %bitcast.78, s32[1024]{0:T(1024)S(1)} %bitcast.77, s32[]{:T(128)} %constant.19.clone.1), kind=kCustom, calls=%fused_computation.59 | custom fusion | bytes 1028 | tf_op jit(solution)/shard_map/scatter | solution.py:36
  28.2 5.7 %all-to-all-done = bf16[4,96,1024]{2,1,0:T(8,128)(2,1)S(1)} async-done(((bf16[4,96,1024]{2,1,0:T(8,128)(2,1)}), bf16[4,96,1024]{2,1,0:T(8,128)(2,1)S(1)}, u32[]{:S(2)}, u32[]{:S(2)}) %all-to-all-start) | async-done | bytes 786464 | tf_op jit(solution)/shard_map/all_to_all | solution.py:27
  33.8 1.2 %gather_fusion = bf16[256,1024]{1,0:T(8,128)(2,1)S(1)} fusion(bf16[384,1024]{1,0:T(8,128)(2,1)S(1)} %bitcast.66, s32[1024]{0:T(1024)S(1)} %pad_clamp_fusion.1), kind=kCustom, calls=%fused_computation | custom fusion | bytes 1049600 | tf_op jit(solution)/shard_map/gather | solution.py:38
  35.0 0.2 reshape.224
  35.2 0.4 copy.30
  35.6 0.3 reshape_reshape.3
  35.9 0.9 copy.20
  36.8 3.5 %all-to-all-start.2 = ((bf16[64,4,8,128]{3,2,0,1:T(8,128)(2,1)}), bf16[64,4,8,128]{3,2,0,1:T(8,128)(2,1)S(1)}, u32[]{:S(2)}, u32[]{:S(2)}) async-start(bf16[64,4,8,128]{3,2,0,1:T(8,128)(2,1)} %copy.20), calls=%async_computation.2 | async-start | bytes 1048576 | tf_op jit(solution)/shard_map/all_to_all | solution.py:65
  40.3 13.7 %all-gather = bf16[1,256,1024]{2,1,0:T(8,128)(2,1)S(1)} all-gather(bf16[1,64,1024]{2,1,0:T(8,128)(2,1)S(1)} %copy-done.1), channel_id=2, replica_groups=mesh['view'=8,'span'=4] {'span'}, dimensions={1}, use_global_device_ids=true | all-gather | bytes 655360 | tf_op jit(solution)/shard_map/all_gather | solution.py:67
  54.0 2.7 %fusion.2 = f32[1024,1024]{1,0:T(8,128)} fusion(bf16[32,8,8,128]{3,2,1,0:T(8,128)(2,1)S(1)} %bitcast.70, bf16[1,256,1024]{2,1,0:T(8,128)(2,1)S(1)} %all-gather), kind=kOutput, calls=%fused_computation.9 | convolution fusion | flops 536870912 | bytes 5242880 | tf_op jit(solution)/shard_map/dot_general | solution.py:68
  56.7 6.0 %convolution_convert_fusion = bf16[64,4096]{1,0:T(8,128)(2,1)S(1)} fusion(bf16[4096,1024]{1,0:T(8,128)(2,1)} %param.7, bf16[1,64,1024]{2,1,0:T(8,128)(2,1)S(1)} %copy-done.1), kind=kOutput, calls=%fused_computation.5 | convolution fusion | flops 537133056 | bytes 9043968 | tf_op jit(solution)/shard_map/dot_general | solution.py:48
  62.8 0.4 reshape.226
  63.1 0.4 copy.29
  63.5 0.2 reshape.267
  63.7 2.6 %scatter_custom_fusion.2 = bf16[384,1024]{1,0:T(8,128)(2,1)} fusion(s32[256]{0:T(256)S(1)} %compare_select_fusion.6, bf16[256,1024]{1,0:T(8,128)(2,1)S(1)} %reshape.267, bf16[]{:T(256)} %constant.15.clone.1), kind=kCustom, calls=%fused_computation.17 | custom fusion | bytes 786434 | tf_op jit(solution)/shard_map/scatter | solution.py:56
  66.3 3.5 %all-to-all-start.1 = ((bf16[4,96,1024]{2,1,0:T(8,128)(2,1)}), bf16[4,96,1024]{2,1,0:T(8,128)(2,1)S(1)}, u32[]{:S(2)}, u32[]{:S(2)}) async-start(bf16[4,96,1024]{2,1,0:T(8,128)(2,1)} %bitcast.14), calls=%async_computation.1 | async-start | bytes 1572864 | tf_op jit(solution)/shard_map/all_to_all | solution.py:57
  69.9 11.4 %psum.14 = f32[1024]{0:T(1024)S(1)} all-reduce(f32[1024]{0:T(1024)S(1)} %convert_reduce_fusion), channel_id=1, replica_groups=mesh['view'=8,'span'=4] {'span'}, use_global_device_ids=true, to_apply=%region_8.9 | all-reduce | flops 1024 | bytes 8192 | tf_op jit(solution)/shard_map/psum | solution.py:72
  81.2 14.5 %psum.15 = f32[1024]{0:T(1024)S(1)} all-reduce(f32[1024]{0:T(1024)S(1)} %psum.14), channel_id=1, replica_groups=mesh['view'=8,'span'=4] {'view'}, use_global_device_ids=true, to_apply=%region_9.10 | all-reduce | flops 1024 | bytes 8192 | tf_op jit(solution)/shard_map/psum | solution.py:72
  95.7 0.6 broadcast_multiply_fusion.1
  96.3 0.4 reshape.225
  96.7 2.0 %gather_fusion.1 = bf16[256,1024]{1,0:T(8,128)(2,1)} fusion(bf16[384,1024]{1,0:T(8,128)(2,1)S(1)} %bitcast.67, s32[1024]{0:T(1024)S(1)} %pad_clamp_fusion), kind=kCustom, calls=%fused_computation.1 | custom fusion | bytes 1049600 | tf_op jit(solution)/shard_map/gather | solution.py:60
  98.7 5.7 %fusion.1 = bf16[1,64,1024]{2,1,0:T(8,128)(2,1)} fusion(bf16[64,4096]{1,0:T(8,128)(2,1)S(1)} %reshape.225, bf16[4096,1024]{1,0:T(8,128)(2,1)} %param.7, f32[1024]{0:T(1024)S(1)} %convert_element_type.18), kind=kOutput, calls=%fused_computation.8 | convolution fusion | flops 537001984 | bytes 9048064 | tf_op jit(solution)/shard_map/dot_general | solution.py:45
  104.4 3.0 %reduce-scatter.2.cloned.1.call-done = f32[128,1024]{1,0:T(8,128)} async-done(((f32[1024,1024]{1,0:T(8,128)}), f32[128,1024]{1,0:T(8,128)}) %reduce-scatter.2.cloned.1.call-update) | async-done | bytes 524304 | tf_op jit(solution)/shard_map/reduce_scatter | solution.py:71
  107.4 1.9 %broadcast_multiply_fusion = f32[128,1024]{1,0:T(8,128)} fusion(f32[128,1024]{1,0:T(8,128)} %reduce-scatter.2.cloned.1.call-done), kind=kLoop, calls=%fused_computation.21 | loop fusion | flops 131072 | bytes 1048576 | tf_op jit(solution)/shard_map/mul | solution.py:74
  (29 shorter events, 0.6 us)
Async XLA Ops:
  7.2 8.1 %copy-start = (bf16[1,256,1024]{2,1,0:T(8,128)(2,1)S(1)}, bf16[1,256,1024]{2,1,0:T(8,128)(2,1)}, u32[]{:S(2)}) copy-start(bf16[1,256,1024]{2,1,0:T(8,128)(2,1)} %param.5) | copy-start | bytes 1572868
  7.2 33.1 %copy-start.1 = (bf16[1,64,1024]{2,1,0:T(8,128)(2,1)S(1)}, bf16[1,64,1024]{2,1,0:T(8,128)(2,1)}, u32[]{:S(2)}) copy-start(bf16[1,64,1024]{2,1,0:T(8,128)(2,1)} %param.9) | copy-start | bytes 393220
  17.8 16.0 %all-to-all-start = ((bf16[4,96,1024]{2,1,0:T(8,128)(2,1)}), bf16[4,96,1024]{2,1,0:T(8,128)(2,1)S(1)}, u32[]{:S(2)}, u32[]{:S(2)}) async-start(bf16[4,96,1024]{2,1,0:T(8,128)(2,1)} %bitcast.6), calls=%async_computation | async-start | bytes 1572864 | tf_op jit(solution)/shard_map/all_to_all | solution.py:27
  36.8 17.2 %all-to-all-start.2 = ((bf16[64,4,8,128]{3,2,0,1:T(8,128)(2,1)}), bf16[64,4,8,128]{3,2,0,1:T(8,128)(2,1)S(1)}, u32[]{:S(2)}, u32[]{:S(2)}) async-start(bf16[64,4,8,128]{3,2,0,1:T(8,128)(2,1)} %copy.20), calls=%async_computation.2 | async-start | bytes 1048576 | tf_op jit(solution)/shard_map/all_to_all | solution.py:65
  40.3 67.1 %reduce-scatter.2.cloned.1.call-start = ((), (), s32[]{:S(2)}) async-start(), calls=%async_computation.4 | async-start | bytes 4718592 | tf_op jit(solution)/shard_map/reduce_scatter | solution.py:71
  56.7 13.1 %copy-start.2 = (bf16[1024]{0:T(1024)(128)(2,1)S(1)}, bf16[1024]{0:T(1024)(128)(2,1)}, u32[]{:S(2)}) copy-start(bf16[1024]{0:T(1024)(128)(2,1)} %param.8) | copy-start | bytes 6148
  66.3 30.4 %all-to-all-start.1 = ((bf16[4,96,1024]{2,1,0:T(8,128)(2,1)}), bf16[4,96,1024]{2,1,0:T(8,128)(2,1)S(1)}, u32[]{:S(2)}, u32[]{:S(2)}) async-start(bf16[4,96,1024]{2,1,0:T(8,128)(2,1)} %bitcast.14), calls=%async_computation.1 | async-start | bytes 1572864 | tf_op jit(solution)/shard_map/all_to_all | solution.py:57
Sparse Core Ops, SparseCore 0:
  56.8 50.5 reduce-scatter.1
